TPU v7x, 32 devices: a whole 2x2x4 slice. The times are simulated.
32 devices in a mesh: parts: 2 (over y), tm: 4 (over z), chan: 4 (over x, core).
Axes of the slice: x: 2, y: 2, z: 4, core: 2. Of those that a mesh axis runs over, the one named last changes fastest.
Arguments:
- records: float32 [512, 1024], P(('parts', 'chan'), 'tm'), parts along dimension 0, may hold values from -8 to 8
- fir_taps: float32 [129], replicated, may hold values from -0.5 to 0.5
- matchings: int32 [2, 4], replicated, may hold values from 0 to 3, as said below
Outputs:
- correlograms: bfloat16 [2, 8, 64, 16448], P(None, ('parts', 'chan'), 'tm'), parts along dimension 1
There are 2 independent parts, one for each index of `parts`. A program takes and returns all parts, laid end to end along the dimension named above; an argument that names none is the same for every part. Nothing has to cross between parts.
Inputs may be any that keep to these rules, and one draw needn't show every extreme that they name: `matchings`: each row sends every group to another group, and following a row from any group visits all 4 groups in one cycle.
All inputs are finite; a program needn't handle non-finite values.
Results may differ from a plain program's by a relative error of at most 0.0049.
Values may be sent and summed in bfloat16 or wider, within the bound.
A program may use at most 64 MiB of HBM per device.

v0:
```python
import math

import jax
import jax.numpy as jnp
from jax import lax
from jax.sharding import PartitionSpec as P

AVG = 65
MAXLAG = 128
LAGS = 257


EPSILON = 1e-05


def extended_2(cells, sides, width):
    for axis, dim in sides:
        count = lax.axis_size(axis)
        ends = count - 1
        head = lax.slice_in_dim(cells, 0, width, axis=dim)
        tail = lax.slice_in_dim(cells, cells.shape[dim] - width, cells.shape[dim], axis=dim)
        cells = jnp.concatenate(
            [
                lax.ppermute(tail, axis, [(i, (i + 1) % count) for i in range(ends)]),
                cells,
                lax.ppermute(head, axis, [((i + 1) % count, i) for i in range(ends)]),
            ],
            axis=dim,
        )
    return cells


def falling(window, row_count):
    leading = window.shape[:-1]
    extended = jnp.concatenate([window, jnp.zeros(leading + (1,), window.dtype)], axis=-1)
    span_width = extended.shape[-1]
    repeated = jnp.broadcast_to(extended[..., None, :], leading + (row_count, span_width))
    repeated = repeated.reshape(leading + (row_count * span_width,))[
        ..., : row_count * (span_width - 1)
    ]
    return repeated.reshape(leading + (row_count, span_width - 1))[..., row_count - 1 :]


def fir_matrix(fir_taps, row_count, col_count):
    tap_count = fir_taps.shape[0]
    padded = jnp.concatenate(
        [
            jnp.zeros((row_count - tap_count,), jnp.float32),
            fir_taps,
            jnp.zeros((col_count - 1,), jnp.float32),
        ]
    )
    return falling(padded, row_count)


def normalize(records, fir_taps):
    tap_half = fir_taps.shape[0] // 2
    avg_half = AVG // 2
    samples_dev = records.shape[1]
    widened = extended_2(records, (("tm", 1),), tap_half + avg_half)
    filtered = jnp.dot(
        widened,
        fir_matrix(fir_taps, samples_dev + 2 * (tap_half + avg_half), samples_dev + 2 * avg_half),
        precision=lax.Precision.HIGHEST,
        preferred_element_type=jnp.float32,
    )
    global_time = (
        lax.axis_index("tm") * samples_dev
        - avg_half
        + lax.iota(jnp.int32, samples_dev + 2 * avg_half)
    )
    inside = (global_time >= 0) & (global_time < samples_dev * lax.axis_size("tm"))
    filtered = jnp.where(inside[None, :], filtered, 0.0)
    magnitude = jnp.abs(filtered)
    rows_at = lax.broadcasted_iota(jnp.int32, (samples_dev + 2 * avg_half, samples_dev), 0)
    cols_at = lax.broadcasted_iota(jnp.int32, (samples_dev + 2 * avg_half, samples_dev), 1)
    band_matrix = ((rows_at >= cols_at) & (rows_at <= cols_at + 2 * avg_half)).astype(jnp.float32)
    local_mean = (
        jnp.dot(
            magnitude,
            band_matrix,
            precision=lax.Precision.HIGHEST,
            preferred_element_type=jnp.float32,
        )
        / AVG
    )
    centre = filtered[:, avg_half : avg_half + samples_dev]
    return (centre / (local_mean + EPSILON)).astype(jnp.bfloat16)


def local(records, fir_taps, matchings):
    normed = normalize(records, fir_taps)
    group_ch, samples_dev = normed.shape
    group_count = lax.axis_size("chan")
    group_index = lax.axis_index("chan")
    match_count = matchings.shape[0]
    every_group = lax.all_gather(normed, "chan", axis=0, tiled=True).reshape(
        group_count, group_ch, samples_dev
    )
    partners = jnp.take(every_group, matchings[:, group_index], axis=0)
    time_count = lax.axis_size("tm")
    scaling = 1.0 / math.sqrt(samples_dev * time_count)
    row_share = group_ch // time_count
    own_rows = lax.all_to_all(normed, "tm", split_axis=0, concat_axis=1, tiled=True)
    padded = jnp.pad(own_rows, ((0, 0), (MAXLAG, MAXLAG)))
    initial = jnp.zeros((match_count, row_share, LAGS, group_ch), jnp.float32)
    incoming = lax.all_gather(partners, "tm", axis=2, tiled=True)
    part_width = incoming.shape[2]
    block_width = math.gcd(part_width, 128)
    block_count = part_width // block_width

    def one_block(block_index, running):
        offset = block_index * block_width
        window = lax.dynamic_slice_in_dim(padded, offset, block_width + 2 * MAXLAG, 1)
        lagged = falling(window, LAGS)
        piece = lax.dynamic_slice_in_dim(incoming, offset, block_width, 2)
        return running + jnp.einsum(
            "ilt,mjt->milj", lagged, piece, preferred_element_type=jnp.float32
        )

    summed = lax.fori_loop(0, block_count, one_block, initial)
    result = (
        (summed * scaling).astype(jnp.bfloat16).reshape(match_count, 1, row_share, LAGS * group_ch)
    )
    return result


def solution(mesh):
    in_specs = (P(("parts", "chan"), "tm"), P(), P())
    out_specs = P(None, ("parts", "chan"), "tm", None)
    return jax.shard_map(local, mesh=mesh, in_specs=in_specs, out_specs=out_specs, check_vma=False)
```

profile of v0, /device:TPU:0, one launch (start us, length us, event | category | flops | bytes accessed | tf_op | source)
XLA Modules:
  0.0 187.4 jit_solution(5128259698536419068)
XLA Ops:
  0.8 4.9 %collective-permute-start = (f32[64,96]{1,0:T(8,128)S(1)}, f32[64,96]{1,0:T(8,128)S(1)}, u32[]{:S(2)}, u32[]{:S(2)}) collective-permute-start(f32[64,96]{1,0:T(8,128)S(1)} %get-tuple-element.108), channel_id=1, source_target_pairs={{0,4},{4,8},{8,12},{1,5},{5,9},{9,13},{2,6},{6,10},{10,14},{3,7},{... | collective-permute-start | bytes 73736 | tf_op jit(solution)/shard_map/ppermute | solution.py:24
  13.2 5.6 %all_gather.6 = bf16[256,256]{1,0:T(8,128)(2,1)S(1)} all-gather(bf16[64,256]{1,0:T(8,128)(2,1)} %fusion.14), channel_id=1, replica_groups=mesh['parts'=2,'tm'=4,'chan'=4] {'chan'}, dimensions={0}, use_global_device_ids=true | all-gather | bytes 163840 | tf_op jit(solution)/shard_map/all_gather | solution.py:97
  18.8 4.9 %all-to-all-start = ((bf16[4,16,256]{2,1,0:T(8,128)(2,1)}), bf16[4,16,256]{2,1,0:T(8,128)(2,1)S(1)}, u32[]{:S(2)}, u32[]{:S(2)}) async-start(bf16[4,16,256]{2,1,0:T(8,128)(2,1)} %bitcast.1), calls=%async_computation | async-start | bytes 65536 | tf_op jit(solution)/shard_map/all_to_all | solution.py:104
  24.4 14.4 %all_gather.7 = bf16[2,64,1024]{2,1,0:T(8,128)(2,1)S(1)} all-gather(bf16[2,64,256]{2,1,0:T(8,128)(2,1)S(1)} %broadcast_select_fusion), channel_id=1, replica_groups=mesh['parts'=2,'tm'=4,'chan'=4] {'tm'}, dimensions={2}, use_global_device_ids=true | all-gather | bytes 327680 | tf_op jit(solution)/shard_map/all_gather | solution.py:107
  38.8 140.0 %while.14 = (s32[]{:T(128)}, f32[2,16,257,64]{2,3,1,0:T(8,128)}, bf16[2,64,1024]{2,1,0:T(8,128)(2,1)S(1)}, bf16[16,1280]{1,0:T(8,128)(2,1)S(1)}, s32[]{:T(128)},...) while((s32[]{:T(128)}, f32[2,16,257,64]{2,3,1,0:T(8,128)}, ...), condition=%wide.region_1.2_spmd.clone, body=%wide.region_0.1_spmd.clone.sunk | while | flops 135794688 | bytes 27517284 | solution.py:121
  41.1 6.5 %reshape.62 = bf16[16,98945]{1,0:T(8,128)(2,1)S(1)} reshape(bf16[16,257,385]{2,1,0:T(8,128)(2,1)} %broadcast_in_dim.60) | data formatting | bytes 6332480 | tf_op jit(solution)/shard_map/while/body/eval_jaxpr/reshape | solution.py:38
  49.5 2.9 %reshape.63 = bf16[16,257,384]{2,1,0:T(8,128)(2,1)S(1)} reshape(bf16[16,98688]{1,0:T(8,128)(2,1)} %slice.55) | data formatting | bytes 6316032 | tf_op jit(solution)/shard_map/while/body/eval_jaxpr/reshape | solution.py:41
  54.7 2.3 %broadcast_in_dim.60 = bf16[16,257,385]{2,1,0:T(8,128)(2,1)} broadcast(bf16[16,385]{1,0:T(8,128)(2,1)S(1)} %concatenate.15), dimensions={0,2} | broadcast | bytes 3178560 | tf_op jit(solution)/shard_map/while/body/eval_jaxpr/broadcast_in_dim | solution.py:37
  57.0 6.5 %reshape.62 = bf16[16,98945]{1,0:T(8,128)(2,1)S(1)} reshape(bf16[16,257,385]{2,1,0:T(8,128)(2,1)} %broadcast_in_dim.60) | data formatting | bytes 6332480 | tf_op jit(solution)/shard_map/while/body/eval_jaxpr/reshape | solution.py:38
  65.4 2.9 %reshape.63 = bf16[16,257,384]{2,1,0:T(8,128)(2,1)S(1)} reshape(bf16[16,98688]{1,0:T(8,128)(2,1)} %slice.55) | data formatting | bytes 6316032 | tf_op jit(solution)/shard_map/while/body/eval_jaxpr/reshape | solution.py:41
  68.3 4.1 %bitcast_add_fusion.2 = f32[2,16,257,64]{2,3,1,0:T(8,128)} fusion(f32[2,16,257,64]{2,3,1,0:T(8,128)} %get-tuple-element.146, pred[]{:T(512)S(6)} %compare.5, bf16[16,257,384]{2,1,0:T(8,128)(2,1)S(1)} %reshape.63, bf16[2,64,1024]{2,1,0:T(8,128)(2,1)S(1)} %get-tuple-element.157, s32[]{:T(128)S(6)} %select_n.48), kind=kOutput, calls=%fused_computation.1.clone.1 | convolution fusion | flops 135794688 | bytes 5324805 | tf_op jit(solution)/shard_map/while/body/eval_jaxpr/ilt,mjt->milj/dot_general | solution.py:117
  72.4 2.3 %broadcast_in_dim.60 = bf16[16,257,385]{2,1,0:T(8,128)(2,1)} broadcast(bf16[16,385]{1,0:T(8,128)(2,1)S(1)} %concatenate.15), dimensions={0,2} | broadcast | bytes 3178560 | tf_op jit(solution)/shard_map/while/body/eval_jaxpr/broadcast_in_dim | solution.py:37
  74.7 6.5 %reshape.62 = bf16[16,98945]{1,0:T(8,128)(2,1)S(1)} reshape(bf16[16,257,385]{2,1,0:T(8,128)(2,1)} %broadcast_in_dim.60) | data formatting | bytes 6332480 | tf_op jit(solution)/shard_map/while/body/eval_jaxpr/reshape | solution.py:38
  83.1 2.9 %reshape.63 = bf16[16,257,384]{2,1,0:T(8,128)(2,1)S(1)} reshape(bf16[16,98688]{1,0:T(8,128)(2,1)} %slice.55) | data formatting | bytes 6316032 | tf_op jit(solution)/shard_map/while/body/eval_jaxpr/reshape | solution.py:41
  86.0 4.2 %bitcast_add_fusion.2 = f32[2,16,257,64]{2,3,1,0:T(8,128)} fusion(f32[2,16,257,64]{2,3,1,0:T(8,128)} %get-tuple-element.146, pred[]{:T(512)S(6)} %compare.5, bf16[16,257,384]{2,1,0:T(8,128)(2,1)S(1)} %reshape.63, bf16[2,64,1024]{2,1,0:T(8,128)(2,1)S(1)} %get-tuple-element.157, s32[]{:T(128)S(6)} %select_n.48), kind=kOutput, calls=%fused_computation.1.clone.1 | convolution fusion | flops 135794688 | bytes 5324805 | tf_op jit(solution)/shard_map/while/body/eval_jaxpr/ilt,mjt->milj/dot_general | solution.py:117
  92.5 6.5 %reshape.62 = bf16[16,98945]{1,0:T(8,128)(2,1)S(1)} reshape(bf16[16,257,385]{2,1,0:T(8,128)(2,1)} %broadcast_in_dim.60) | data formatting | bytes 6332480 | tf_op jit(solution)/shard_map/while/body/eval_jaxpr/reshape | solution.py:38
  100.9 2.9 %reshape.63 = bf16[16,257,384]{2,1,0:T(8,128)(2,1)S(1)} reshape(bf16[16,98688]{1,0:T(8,128)(2,1)} %slice.55) | data formatting | bytes 6316032 | tf_op jit(solution)/shard_map/while/body/eval_jaxpr/reshape | solution.py:41
  103.8 4.2 %bitcast_add_fusion.2 = f32[2,16,257,64]{2,3,1,0:T(8,128)} fusion(f32[2,16,257,64]{2,3,1,0:T(8,128)} %get-tuple-element.146, pred[]{:T(512)S(6)} %compare.5, bf16[16,257,384]{2,1,0:T(8,128)(2,1)S(1)} %reshape.63, bf16[2,64,1024]{2,1,0:T(8,128)(2,1)S(1)} %get-tuple-element.157, s32[]{:T(128)S(6)} %select_n.48), kind=kOutput, calls=%fused_computation.1.clone.1 | convolution fusion | flops 135794688 | bytes 5324805 | tf_op jit(solution)/shard_map/while/body/eval_jaxpr/ilt,mjt->milj/dot_general | solution.py:117
  110.2 6.5 %reshape.62 = bf16[16,98945]{1,0:T(8,128)(2,1)S(1)} reshape(bf16[16,257,385]{2,1,0:T(8,128)(2,1)} %broadcast_in_dim.60) | data formatting | bytes 6332480 | tf_op jit(solution)/shard_map/while/body/eval_jaxpr/reshape | solution.py:38
  118.6 2.9 %reshape.63 = bf16[16,257,384]{2,1,0:T(8,128)(2,1)S(1)} reshape(bf16[16,98688]{1,0:T(8,128)(2,1)} %slice.55) | data formatting | bytes 6316032 | tf_op jit(solution)/shard_map/while/body/eval_jaxpr/reshape | solution.py:41
  121.5 4.2 %bitcast_add_fusion.2 = f32[2,16,257,64]{2,3,1,0:T(8,128)} fusion(f32[2,16,257,64]{2,3,1,0:T(8,128)} %get-tuple-element.146, pred[]{:T(512)S(6)} %compare.5, bf16[16,257,384]{2,1,0:T(8,128)(2,1)S(1)} %reshape.63, bf16[2,64,1024]{2,1,0:T(8,128)(2,1)S(1)} %get-tuple-element.157, s32[]{:T(128)S(6)} %select_n.48), kind=kOutput, calls=%fused_computation.1.clone.1 | convolution fusion | flops 135794688 | bytes 5324805 | tf_op jit(solution)/shard_map/while/body/eval_jaxpr/ilt,mjt->milj/dot_general | solution.py:117
  127.9 6.5 %reshape.62 = bf16[16,98945]{1,0:T(8,128)(2,1)S(1)} reshape(bf16[16,257,385]{2,1,0:T(8,128)(2,1)} %broadcast_in_dim.60) | data formatting | bytes 6332480 | tf_op jit(solution)/shard_map/while/body/eval_jaxpr/reshape | solution.py:38
  136.3 2.9 %reshape.63 = bf16[16,257,384]{2,1,0:T(8,128)(2,1)S(1)} reshape(bf16[16,98688]{1,0:T(8,128)(2,1)} %slice.55) | data formatting | bytes 6316032 | tf_op jit(solution)/shard_map/while/body/eval_jaxpr/reshape | solution.py:41
  139.2 4.1 %bitcast_add_fusion.2 = f32[2,16,257,64]{2,3,1,0:T(8,128)} fusion(f32[2,16,257,64]{2,3,1,0:T(8,128)} %get-tuple-element.146, pred[]{:T(512)S(6)} %compare.5, bf16[16,257,384]{2,1,0:T(8,128)(2,1)S(1)} %reshape.63, bf16[2,64,1024]{2,1,0:T(8,128)(2,1)S(1)} %get-tuple-element.157, s32[]{:T(128)S(6)} %select_n.48), kind=kOutput, calls=%fused_computation.1.clone.1 | convolution fusion | flops 135794688 | bytes 5324805 | tf_op jit(solution)/shard_map/while/body/eval_jaxpr/ilt,mjt->milj/dot_general | solution.py:117
  145.7 6.5 %reshape.62 = bf16[16,98945]{1,0:T(8,128)(2,1)S(1)} reshape(bf16[16,257,385]{2,1,0:T(8,128)(2,1)} %broadcast_in_dim.60) | data formatting | bytes 6332480 | tf_op jit(solution)/shard_map/while/body/eval_jaxpr/reshape | solution.py:38
  154.1 2.9 %reshape.63 = bf16[16,257,384]{2,1,0:T(8,128)(2,1)S(1)} reshape(bf16[16,98688]{1,0:T(8,128)(2,1)} %slice.55) | data formatting | bytes 6316032 | tf_op jit(solution)/shard_map/while/body/eval_jaxpr/reshape | solution.py:41
  157.0 4.2 %bitcast_add_fusion.2 = f32[2,16,257,64]{2,3,1,0:T(8,128)} fusion(f32[2,16,257,64]{2,3,1,0:T(8,128)} %get-tuple-element.146, pred[]{:T(512)S(6)} %compare.5, bf16[16,257,384]{2,1,0:T(8,128)(2,1)S(1)} %reshape.63, bf16[2,64,1024]{2,1,0:T(8,128)(2,1)S(1)} %get-tuple-element.157, s32[]{:T(128)S(6)} %select_n.48), kind=kOutput, calls=%fused_computation.1.clone.1 | convolution fusion | flops 135794688 | bytes 5324805 | tf_op jit(solution)/shard_map/while/body/eval_jaxpr/ilt,mjt->milj/dot_general | solution.py:117
  163.4 6.5 %reshape.62 = bf16[16,98945]{1,0:T(8,128)(2,1)S(1)} reshape(bf16[16,257,385]{2,1,0:T(8,128)(2,1)} %broadcast_in_dim.60) | data formatting | bytes 6332480 | tf_op jit(solution)/shard_map/while/body/eval_jaxpr/reshape | solution.py:38
  171.8 2.9 %reshape.63 = bf16[16,257,384]{2,1,0:T(8,128)(2,1)S(1)} reshape(bf16[16,98688]{1,0:T(8,128)(2,1)} %slice.55) | data formatting | bytes 6316032 | tf_op jit(solution)/shard_map/while/body/eval_jaxpr/reshape | solution.py:41
  174.7 4.1 %bitcast_add_fusion.2 = f32[2,16,257,64]{2,3,1,0:T(8,128)} fusion(f32[2,16,257,64]{2,3,1,0:T(8,128)} %get-tuple-element.146, pred[]{:T(512)S(6)} %compare.5, bf16[16,257,384]{2,1,0:T(8,128)(2,1)S(1)} %reshape.63, bf16[2,64,1024]{2,1,0:T(8,128)(2,1)S(1)} %get-tuple-element.157, s32[]{:T(128)S(6)} %select_n.48), kind=kOutput, calls=%fused_computation.1.clone.1 | convolution fusion | flops 135794688 | bytes 5324805 | tf_op jit(solution)/shard_map/while/body/eval_jaxpr/ilt,mjt->milj/dot_general | solution.py:117
  178.8 3.4 %multiply_convert_fusion = bf16[2,16,257,64]{2,3,1,0:T(8,128)(2,1)} fusion(f32[2,16,257,64]{2,3,1,0:T(8,128)} %get-tuple-element.84), kind=kLoop, calls=%fused_computation.7 | loop fusion | flops 1052672 | bytes 3158016 | tf_op jit(solution)/shard_map/convert_element_type | solution.py:123
  182.3 3.0 %copy.7 = bf16[2,16,257,64]{3,2,1,0:T(8,128)(2,1)S(1)} copy(bf16[2,16,257,64]{2,3,1,0:T(8,128)(2,1)} %multiply_convert_fusion) | data formatting | bytes 2105344 | tf_op jit(solution)/shard_map/convert_element_type | solution.py:123
  (58 shorter events, 41.7 us)
Async XLA Ops:
  0.8 9.7 %collective-permute-start = (f32[64,96]{1,0:T(8,128)S(1)}, f32[64,96]{1,0:T(8,128)S(1)}, u32[]{:S(2)}, u32[]{:S(2)}) collective-permute-start(f32[64,96]{1,0:T(8,128)S(1)} %get-tuple-element.108), channel_id=1, source_target_pairs={{0,4},{4,8},{8,12},{1,5},{5,9},{9,13},{2,6},{6,10},{10,14},{3,7},{... | collective-permute-start | bytes 73736 | tf_op jit(solution)/shard_map/ppermute | solution.py:24
  5.8 5.8 %collective-permute-start.1 = (f32[64,96]{1,0:T(8,128)S(1)}, f32[64,96]{1,0:T(8,128)S(1)}, u32[]{:S(2)}, u32[]{:S(2)}) collective-permute-start(f32[64,96]{1,0:T(8,128)S(1)} %get-tuple-element.109), channel_id=1, source_target_pairs={{4,0},{8,4},{12,8},{5,1},{9,5},{13,9},{6,2},{10,6},{14,10},{7,3},{... | collective-permute-start | bytes 73736 | tf_op jit(solution)/shard_map/ppermute | solution.py:26
  8.8 1.6 copy-start.1
  8.8 2.8 %copy-start = (f32[64,256]{1,0:T(8,128)S(1)}, f32[64,256]{1,0:T(8,128)}, u32[]{:S(2)}) copy-start(f32[64,256]{1,0:T(8,128)} %param.5) | copy-start | bytes 196612
  18.8 20.0 %all-to-all-start = ((bf16[4,16,256]{2,1,0:T(8,128)(2,1)}), bf16[4,16,256]{2,1,0:T(8,128)(2,1)S(1)}, u32[]{:S(2)}, u32[]{:S(2)}) async-start(bf16[4,16,256]{2,1,0:T(8,128)(2,1)} %bitcast.1), calls=%async_computation | async-start | bytes 65536 | tf_op jit(solution)/shard_map/all_to_all | solution.py:104
where the time goes:
time: 188 us; the launch traced here: 187 us
  local copies, waits for them, and re-layouts  117 us (62%)
  matrix products  32.9 us (18%)
  blocking collectives  20 us (11%)
  starting transfers between devices  11.1 us (6%)
  other arithmetic  5.36 us (3%)
    reshape x9, local copies, waits for them, and re-layouts, falling(): repeated.reshape(leading + (row_count * span_width,))  52.5 us
    dot_general x8, matrix products, one_block(): jnp.einsum('ilt,mjt->milj', lagged, piece, preferred_element_type=jnp.flo...  31.3 us
    reshape x9, local copies, waits for them, and re-layouts, falling(): repeated.reshape(leading + (row_count, span_width - 1))[..., row_count - 1:]  24.4 us
    broadcast_in_dim x9, local copies, waits for them, and re-layouts, falling(): jnp.broadcast_to(extended[..., None, :], leading + (row_count, span_width))  18.3 us
    slice x8, local copies, waits for them, and re-layouts, falling(): repeated.reshape(leading + (row_count * span_width,))  14.8 us
    all_gather x1, blocking collectives, local(): incoming = lax.all_gather(partners, 'tm', axis=2, tiled=True)  14.4 us
    all_gather x1, blocking collectives, local(): lax.all_gather(normed, 'chan', axis=0, tiled=True)  5.61 us
    ppermute x1, starting transfers between devices, extended_2(): lax.ppermute(tail, axis, [(i, (i + 1) % count) for i in range(ends)])  4.95 us
  transfers between devices with their start and end apart: 3, of which 1 were waited for; matrix products, arithmetic and copies ran while one was open for 2% of the time, Pallas kernels for 0%

commit v1 on v0

--- a/solution.py
+++ b/solution.py
@@ -1,8 +1,11 @@
+import functools
 import math
 
 import jax
 import jax.numpy as jnp
 from jax import lax
+from jax.experimental import pallas as pl
+from jax.experimental.pallas import tpu as pltpu
 from jax.sharding import PartitionSpec as P
 
 AVG = 65
@@ -88,6 +91,43 @@
     return (centre / (local_mean + EPSILON)).astype(jnp.bfloat16)
 
 
+def correlate(row_share, scaling, own_ref, partners_ref, out_ref):
+    rows, samples = own_ref.shape
+    match_count, group_ch, _ = partners_ref.shape
+    depth = samples + MAXLAG
+    width = samples + 2 * MAXLAG
+    margin = jnp.zeros((rows, MAXLAG), jnp.bfloat16)
+    own = jnp.concatenate([margin, own_ref[...], margin], axis=1).astype(jnp.float32)
+    tail = jnp.zeros((group_ch, MAXLAG), jnp.bfloat16)
+    weights = []
+    for match in range(match_count):
+        ahead = jnp.concatenate([partners_ref[match], tail], axis=1)
+        behind = pltpu.roll(ahead.astype(jnp.float32), 1, 1).astype(jnp.bfloat16)
+        weights += [behind, ahead]
+    weights = jnp.concatenate(weights, axis=0)
+    pair = 2 * group_ch
+    per_chunk = 16
+    for first in range(0, LAGS, 2 * per_chunk):
+        lags = range(first, min(first + 2 * per_chunk, LAGS), 2)
+        lagged = jnp.concatenate(
+            [
+                pltpu.roll(own, (lag - (2 * MAXLAG - 1)) % width, 1)[:, :depth].astype(jnp.bfloat16)
+                for lag in lags
+            ],
+            axis=0,
+        )
+        summed = lax.dot_general(
+            lagged, weights, (((1,), (1,)), ((), ())), preferred_element_type=jnp.float32
+        )
+        scaled = (summed * scaling).astype(jnp.bfloat16)
+        for at, lag in enumerate(lags):
+            span = min(pair, (LAGS - lag) * group_ch)
+            for match in range(match_count):
+                out_ref[match, 0, :, lag * group_ch : lag * group_ch + span] = scaled[
+                    at * rows : at * rows + row_share, match * pair : match * pair + span
+                ]
+
+
 def local(records, fir_taps, matchings):
     normed = normalize(records, fir_taps)
     group_ch, samples_dev = normed.shape
@@ -102,27 +142,17 @@
     scaling = 1.0 / math.sqrt(samples_dev * time_count)
     row_share = group_ch // time_count
     own_rows = lax.all_to_all(normed, "tm", split_axis=0, concat_axis=1, tiled=True)
-    padded = jnp.pad(own_rows, ((0, 0), (MAXLAG, MAXLAG)))
-    initial = jnp.zeros((match_count, row_share, LAGS, group_ch), jnp.float32)
     incoming = lax.all_gather(partners, "tm", axis=2, tiled=True)
-    part_width = incoming.shape[2]
-    block_width = math.gcd(part_width, 128)
-    block_count = part_width // block_width
-
-    def one_block(block_index, running):
-        offset = block_index * block_width
-        window = lax.dynamic_slice_in_dim(padded, offset, block_width + 2 * MAXLAG, 1)
-        lagged = falling(window, LAGS)
-        piece = lax.dynamic_slice_in_dim(incoming, offset, block_width, 2)
-        return running + jnp.einsum(
-            "ilt,mjt->milj", lagged, piece, preferred_element_type=jnp.float32
-        )
-
-    summed = lax.fori_loop(0, block_count, one_block, initial)
-    result = (
-        (summed * scaling).astype(jnp.bfloat16).reshape(match_count, 1, row_share, LAGS * group_ch)
-    )
-    return result
+    rows = -(-row_share // 16) * 16
+    own_rows = jnp.pad(own_rows, ((0, rows - row_share), (0, 0)))
+    return pl.pallas_call(
+        functools.partial(correlate, row_share, scaling),
+        out_shape=jax.ShapeDtypeStruct(
+            (match_count, 1, row_share, LAGS * group_ch), jnp.bfloat16
+        ),
+        in_specs=[pl.BlockSpec(memory_space=pltpu.VMEM)] * 2,
+        out_specs=pl.BlockSpec(memory_space=pltpu.VMEM),
+    )(own_rows, incoming)
 
 
 def solution(mesh):

time: 188 us -> 43.2 us (0.23)
  local copies, waits for them, and re-layouts: 117 us -> 3.54 us
  matrix products: 32.9 us -> 1.59 us
  Pallas kernels: 0 us -> 3.73 us
  other arithmetic: 5.36 us -> 1.91 us
    reshape x9 -> x1, local copies, waits for them, and re-layouts: 52.5 us -> 0.09 us  [falling(): repeated.reshape(leading + (row_count * span_width,))]
    dot_general x8 -> x0, matrix products: 31.3 us -> none  [one_block(): jnp.einsum('ilt,mjt->milj', lagged, piece, preferred_element_type=jnp.flo...]
    reshape x9 -> x1, local copies, waits for them, and re-layouts: 24.4 us -> 1.34 us  [falling(): repeated.reshape(leading + (row_count, span_width - 1))[..., row_count - 1:]]
    broadcast_in_dim x9 -> x1, local copies, waits for them, and re-layouts: 18.3 us -> 0.09 us  [falling(): jnp.broadcast_to(extended[..., None, :], leading + (row_count, span_width))]
    slice x8 -> x0, local copies, waits for them, and re-layouts: 14.8 us -> none  [falling(): repeated.reshape(leading + (row_count * span_width,))]
    pallas_call x0 -> x1, Pallas kernels: none -> 3.73 us  [local(): pl.pallas_call(functools.partial(correlate, row_share, scaling), out_shap...]
    convert_element_type x1 -> x0, other arithmetic: 3.45 us -> none  [local(): (summed * scaling).astype(jnp.bfloat16)]
    convert_element_type x1 -> x0, local copies, waits for them, and re-layouts: 3.03 us -> none  [local(): (summed * scaling).astype(jnp.bfloat16)]
  transfers between devices with their start and end apart: 3 -> 3, of which waited for: 1 -> 0; matrix products, arithmetic and copies ran while one was open for 2% -> 9% of each run, Pallas kernels for 0% -> 0%
where the time goes in v1:
time: 43.2 us; the launch traced here: 42.9 us
  blocking collectives  20.9 us (48%)
  starting transfers between devices  11.1 us (26%)
  Pallas kernels  3.73 us (9%)
  local copies, waits for them, and re-layouts  3.54 us (8%)
  other arithmetic  1.91 us (4%)
  matrix products  1.59 us (4%)
    all_gather x1, blocking collectives, local(): incoming = lax.all_gather(partners, 'tm', axis=2, tiled=True)  15.2 us
    all_gather x1, blocking collectives, local(): lax.all_gather(normed, 'chan', axis=0, tiled=True)  5.67 us
    ppermute x1, starting transfers between devices, extended_2(): lax.ppermute(tail, axis, [(i, (i + 1) % count) for i in range(ends)])  5.59 us
    all_to_all x1, starting transfers between devices, local(): lax.all_to_all(normed, 'tm', split_axis=0, concat_axis=1, tiled=True)  4.24 us
    pallas_call x1, Pallas kernels, local(): pl.pallas_call(functools.partial(correlate, row_share, scaling), out_shap...  3.73 us
    reshape x1, local copies, waits for them, and re-layouts, falling(): repeated.reshape(leading + (row_count, span_width - 1))[..., row_count - 1:]  1.34 us
    ppermute x1, starting transfers between devices, extended_2(): lax.ppermute(head, axis, [((i + 1) % count, i) for i in range(ends)])  1.28 us
    select_n x2, other arithmetic, local(): partners = jnp.take(every_group, matchings[:, group_index], axis=0)  0.95 us
  transfers between devices with their start and end apart: 3, of which 0 were waited for; matrix products, arithmetic and copies ran while one was open for 9% of the time, Pallas kernels for 0%

profile of v1, /device:TPU:0, one launch (start us, length us, event | category | flops | bytes accessed | tf_op | source)
XLA Modules:
  0.0 42.9 jit_solution(15938514557480396269)
XLA Ops:
  0.0 0.8 %fusion.21 = (f32[64,96]{1,0:T(8,128)S(1)}, f32[64,96]{1,0:T(8,128)S(1)}) fusion(f32[64,256]{1,0:T(8,128)} %param.3), kind=kLoop, calls=%fused_computation.29 | loop fusion | bytes 98304 | tf_op jit(solution)/shard_map/slice | solution.py:24
  0.8 1.3 %collective-permute-start.1 = (f32[64,96]{1,0:T(8,128)S(1)}, f32[64,96]{1,0:T(8,128)S(1)}, u32[]{:S(2)}, u32[]{:S(2)}) collective-permute-start(f32[64,96]{1,0:T(8,128)S(1)} %get-tuple-element.6), channel_id=1, source_target_pairs={{4,0},{8,4},{12,8},{5,1},{9,5},{13,9},{6,2},{10,6},{14,10},{7,3},{... | collective-permute-start | bytes 73736 | tf_op jit(solution)/shard_map/ppermute | solution.py:29
  2.1 5.6 %collective-permute-start = (f32[64,96]{1,0:T(8,128)S(1)}, f32[64,96]{1,0:T(8,128)S(1)}, u32[]{:S(2)}, u32[]{:S(2)}) collective-permute-start(f32[64,96]{1,0:T(8,128)S(1)} %get-tuple-element.5), channel_id=1, source_target_pairs={{0,4},{4,8},{8,12},{1,5},{5,9},{9,13},{2,6},{6,10},{10,14},{3,7},{... | collective-permute-start | bytes 73736 | tf_op jit(solution)/shard_map/ppermute | solution.py:27
  7.8 0.9 %fusion.20 = s32[2]{0:T(128)S(1)} fusion(s32[2,4]{1,0:T(2,128)} %param.5, s32[]{:T(128)S(6)} %select_n.19), kind=kLoop, calls=%fused_computation.28 | loop fusion | flops 6 | bytes 20 | tf_op jit(solution)/shard_map/jit(_take)/jit(_where)/select_n | solution.py:140
  8.6 0.8 %pad_maximum_fusion = f32[768]{0:T(1024)S(1)} fusion(f32[1]{0:T(128)} %constant.12.clone.1, f32[319]{0:T(512)S(1)} %broadcast.35, f32[129]{0:T(256)} %param.4), kind=kLoop, calls=%fused_computation.19 | loop fusion | flops 2304 | bytes 4868 | tf_op jit(solution)/shard_map/concatenate | solution.py:38
  9.4 0.1 broadcast_in_dim.30
  9.5 0.1 reshape.24
  9.6 0.0 copy-start.1
  9.6 0.0 copy-start
  9.6 1.3 %reshape.25 = f32[448,767]{1,0:T(8,128)S(1)} reshape(f32[343616]{0:T(1024)S(1)} %bitcast.6) | data formatting | bytes 2748928 | tf_op jit(solution)/shard_map/reshape | solution.py:44
  11.0 0.0 copy-done.1
  11.0 0.2 and_reduce_fusion
  11.2 0.0 collective-permute-done.1
  11.2 0.0 collective-permute-done
  11.2 0.0 copy-done
  11.2 0.7 %convolution_select_fusion = f32[64,320]{1,0:T(8,128)S(1)} fusion(f32[448,767]{1,0:T(8,128)S(1)} %reshape.25, f32[64,96]{1,0:T(8,128)S(1)} %collective-permute-done.1, f32[64,256]{1,0:T(8,128)S(1)} %copy-done, f32[64,96]{1,0:T(8,128)S(1)} %collective-permute-done, pred[320]{0:T(512)(128)(4,1)S(1)} %fusion.18), kind=kOutput, calls=%fused_computation.1 | convolution fusion | flops 110178304 | bytes 901632 | tf_op jit(solution)/shard_map/dot_general | solution.py:64
  11.9 0.9 %fusion.11 = bf16[64,256]{1,0:T(8,128)(2,1)} fusion(f32[64,320]{1,0:T(8,128)S(1)} %convolution_select_fusion, s32[256]{0:T(256)S(1)} %iota_add_fusion.1), kind=kOutput, calls=%fused_computation.16 | convolution fusion | flops 63246336 | bytes 197632 | tf_op jit(solution)/shard_map/dot_general | solution.py:82
  12.8 5.7 %all_gather.6 = bf16[256,256]{1,0:T(8,128)(2,1)S(1)} all-gather(bf16[64,256]{1,0:T(8,128)(2,1)} %fusion.11), channel_id=1, replica_groups=mesh['parts'=2,'tm'=4,'chan'=4] {'chan'}, dimensions={0}, use_global_device_ids=true | all-gather | bytes 163840 | tf_op jit(solution)/shard_map/all_gather | solution.py:137
  18.5 4.2 %all-to-all-start = ((bf16[4,16,256]{2,1,0:T(8,128)(2,1)}), bf16[4,16,256]{2,1,0:T(8,128)(2,1)S(1)}, u32[]{:S(2)}, u32[]{:S(2)}) async-start(bf16[4,16,256]{2,1,0:T(8,128)(2,1)} %bitcast), calls=%async_computation | async-start | bytes 65536 | tf_op jit(solution)/shard_map/all_to_all | solution.py:144
  22.7 0.5 %gather_fusion = bf16[2,64,256]{2,1,0:T(8,128)(2,1)S(1)} fusion(bf16[4,64,256]{2,1,0:T(8,128)(2,1)S(1)} %bitcast.7, s32[1024]{0:T(1024)S(1)} %pad_clamp_fusion), kind=kCustom, calls=%fused_computation | custom fusion | bytes 131080 | tf_op jit(solution)/shard_map/jit(_take)/gather | solution.py:140
  23.3 0.1 broadcast_select_fusion
  23.3 15.2 %all_gather.7.partners_ref = bf16[2,64,1024]{2,1,0:T(8,128)(2,1)} all-gather(bf16[2,64,256]{2,1,0:T(8,128)(2,1)S(1)} %broadcast_select_fusion), channel_id=1, replica_groups=mesh['parts'=2,'tm'=4,'chan'=4] {'tm'}, dimensions={2}, use_global_device_ids=true | all-gather | bytes 327680 | tf_op jit(solution)/shard_map/all_gather | solution.py:145
  38.5 0.0 all-to-all-done
  38.5 0.6 %copy.6 = bf16[4,2,8,256]{3,2,0,1:T(8,128)(2,1)} copy(bf16[4,2,8,256]{3,2,1,0:T(8,128)(2,1)S(1)} %bitcast.8) | data formatting | bytes 65536 | tf_op jit(solution)/shard_map/all_to_all | solution.py:144
  39.1 3.7 %shard_map.37 = bf16[2,1,16,16448]{3,2,1,0:T(8,128)(2,1)} custom-call(bf16[16,1024]{1,0:T(8,128)(2,1)} %bitcast.9, bf16[2,64,1024]{2,1,0:T(8,128)(2,1)} %all_gather.7.partners_ref), custom_call_target="tpu_custom_call" | custom-call | tf_op jit(solution)/shard_map/pallas_call | solution.py:148
  (4 shorter events, 0.0 us)
Async XLA Ops:
  0.8 10.3 %collective-permute-start.1 = (f32[64,96]{1,0:T(8,128)S(1)}, f32[64,96]{1,0:T(8,128)S(1)}, u32[]{:S(2)}, u32[]{:S(2)}) collective-permute-start(f32[64,96]{1,0:T(8,128)S(1)} %get-tuple-element.6), channel_id=1, source_target_pairs={{4,0},{8,4},{12,8},{5,1},{9,5},{13,9},{6,2},{10,6},{14,10},{7,3},{... | collective-permute-start | bytes 73736 | tf_op jit(solution)/shard_map/ppermute | solution.py:29
  2.1 9.0 %collective-permute-start = (f32[64,96]{1,0:T(8,128)S(1)}, f32[64,96]{1,0:T(8,128)S(1)}, u32[]{:S(2)}, u32[]{:S(2)}) collective-permute-start(f32[64,96]{1,0:T(8,128)S(1)} %get-tuple-element.5), channel_id=1, source_target_pairs={{0,4},{4,8},{8,12},{1,5},{5,9},{9,13},{2,6},{6,10},{10,14},{3,7},{... | collective-permute-start | bytes 73736 | tf_op jit(solution)/shard_map/ppermute | solution.py:27
  9.6 1.4 %copy-start.1 = (s32[2,4]{1,0:T(2,128)S(1)}, s32[2,4]{1,0:T(2,128)}, u32[]{:S(2)}) copy-start(s32[2,4]{1,0:T(2,128)} %param.5) | copy-start | bytes 100
  9.6 1.6 %copy-start = (f32[64,256]{1,0:T(8,128)S(1)}, f32[64,256]{1,0:T(8,128)}, u32[]{:S(2)}) copy-start(f32[64,256]{1,0:T(8,128)} %param.3) | copy-start | bytes 196612
  18.5 20.1 %all-to-all-start = ((bf16[4,16,256]{2,1,0:T(8,128)(2,1)}), bf16[4,16,256]{2,1,0:T(8,128)(2,1)S(1)}, u32[]{:S(2)}, u32[]{:S(2)}) async-start(bf16[4,16,256]{2,1,0:T(8,128)(2,1)} %bitcast), calls=%async_computation | async-start | bytes 65536 | tf_op jit(solution)/shard_map/all_to_all | solution.py:144

commit v2 on v1

v2 whole, which is shorter than its diff:
```python
import functools
import math

import jax
import jax.numpy as jnp
from jax import lax
from jax.experimental import pallas as pl
from jax.experimental.pallas import tpu as pltpu
from jax.sharding import PartitionSpec as P

AVG = 65
MAXLAG = 128
LAGS = 257
HALO = 128
CORES = 2

EPSILON = 1e-05


def split(values):
    high = values.astype(jnp.bfloat16)
    low = (values - high.astype(jnp.float32)).astype(jnp.bfloat16)
    return high, low


def flipped(at, step, count):
    if count & (count - 1):
        return lax.rem(at + step, count)
    bit = 1
    while bit <= step:
        if step & bit:
            at = at + bit * (1 - 2 * lax.rem(at // bit, 2))
        bit *= 2
    return at


def gather(
    time_count,
    group_count,
    records_ref,
    taps_ref,
    every_ref,
    wide,
    taps_row,
    halo_send,
    halo_recv,
    send_sem,
    recv_sem,
):
    time_at, chan_at = lax.axis_index("tm"), lax.axis_index("chan")
    channels, samples = records_ref.shape
    width = samples + 2 * HALO
    chips = group_count // CORES
    chip_at, core_at = chan_at // CORES, lax.rem(chan_at, CORES)
    sibling = {"chan": chan_at + 1 - 2 * core_at}
    times = [flipped(time_at, step, time_count) for step in range(time_count)]
    others = [
        lax.rem(chip_at + step, chips) * CORES + core_at for step in range(1, chips)
    ]

    barrier = pltpu.get_barrier_semaphore()
    peers = [{"tm": at} for at in times[1:]] + [{"chan": at} for at in others] + [sibling]
    for peer in peers:
        pl.semaphore_signal(barrier, inc=1, device_id=peer)

    taps_row[...] = jnp.zeros_like(taps_row)
    taps_row[0:1, 0 : taps_ref.shape[1]] = taps_ref[...]
    tap_half = taps_ref.shape[1] // 2
    fir = pltpu.roll(
        jnp.broadcast_to(taps_row[0:1, :], (width, width)),
        width - tap_half,
        1,
        stride=1,
        stride_axis=0,
    )
    fir_high, fir_low = split(fir)
    pl.semaphore_wait(barrier, len(peers))

    def halo(source, target, side, to):
        return pltpu.make_async_remote_copy(
            src_ref=records_ref.at[:, source],
            dst_ref=wide.at[:, target],
            send_sem=halo_send.at[side],
            recv_sem=halo_recv.at[side],
            device_id={"tm": to},
        )

    to_next = halo(pl.ds(samples - HALO, HALO), pl.ds(0, HALO), 0, time_at + 1)
    to_last = halo(pl.ds(0, HALO), pl.ds(samples + HALO, HALO), 1, time_at - 1)
    has_next, has_last = time_at < time_count - 1, time_at > 0
    pl.when(has_next)(to_next.start)
    pl.when(has_last)(to_last.start)
    wide[:, HALO : HALO + samples] = records_ref[...]

    @pl.when(jnp.logical_not(has_last))
    def _():
        wide[:, 0:HALO] = jnp.zeros((channels, HALO), jnp.float32)

    @pl.when(jnp.logical_not(has_next))
    def _():
        wide[:, samples + HALO : width] = jnp.zeros((channels, HALO), jnp.float32)

    pl.when(has_last)(to_next.wait_recv)
    pl.when(has_next)(to_last.wait_recv)

    high, low = split(wide[...])
    both = jnp.dot(
        jnp.concatenate([high, low], axis=0), fir_high, preferred_element_type=jnp.float32
    )
    filtered = (
        both[0:channels]
        + both[channels : 2 * channels]
        + jnp.dot(high, fir_low, preferred_element_type=jnp.float32)
    )
    at = time_at * samples - HALO + lax.broadcasted_iota(jnp.int32, (channels, width), 1)
    filtered = jnp.where((at >= 0) & (at < samples * time_count), filtered, 0.0)
    rows_at = lax.broadcasted_iota(jnp.int32, (width, samples), 0)
    cols_at = lax.broadcasted_iota(jnp.int32, (width, samples), 1) + HALO
    band = (jnp.abs(rows_at - cols_at) <= AVG // 2).astype(jnp.float32).astype(jnp.bfloat16)
    summed = jnp.dot(
        jnp.concatenate(split(jnp.abs(filtered)), axis=0), band, preferred_element_type=jnp.float32
    )
    local_mean = (summed[0:channels] + summed[channels : 2 * channels]) / AVG
    centre = filtered[:, HALO : HALO + samples]
    every_ref[chan_at, time_at] = (centre / (local_mean + EPSILON)).astype(jnp.bfloat16)

    sent = []

    def push(chan_from, time_from, to):
        block = every_ref.at[chan_from, time_from]
        copy = pltpu.make_async_remote_copy(
            src_ref=block,
            dst_ref=block,
            send_sem=send_sem.at[len(sent)],
            recv_sem=recv_sem.at[chan_from, time_from],
            device_id=to,
        )
        copy.start()
        sent.append(copy)

    def arrived(chan_from, time_from):
        block = every_ref.at[chan_from, time_from]
        pltpu.make_async_remote_copy(
            src_ref=block,
            dst_ref=block,
            send_sem=send_sem.at[0],
            recv_sem=recv_sem.at[chan_from, time_from],
            device_id=sibling,
        ).wait_recv()

    for time_to in reversed(times[1:]):
        push(chan_at, time_at, {"tm": time_to})
    for step, time_from in enumerate(times):
        if step:
            arrived(chan_at, time_from)
        for chan_to in others:
            push(chan_at, time_from, {"chan": chan_to})
        push(chan_at, time_from, sibling)
        if step:
            for chan_from in others:
                arrived(chan_from, times[step - 1])
                push(chan_from, times[step - 1], sibling)
    for chan_from in others:
        arrived(chan_from, times[-1])
        push(chan_from, times[-1], sibling)
    for time_from in times:
        for chan_from in [chan_at] + others:
            arrived(chan_from + 1 - 2 * core_at, time_from)
    for copy in sent:
        copy.wait_send()
    pl.when(has_next)(to_next.wait_send)
    pl.when(has_last)(to_last.wait_send)


def correlate(row_share, scaling, matchings_ref, every_ref, out_ref):
    _, time_count, group_ch, samples_dev = every_ref.shape
    match_count = matchings_ref.shape[0]
    samples = time_count * samples_dev
    chan_at, time_at = lax.axis_index("chan"), lax.axis_index("tm")
    depth = samples + MAXLAG
    width = samples + 2 * MAXLAG
    rows = -(-row_share // 16) * 16
    row_at = time_at * row_share
    start = pl.multiple_of(row_at // rows * rows, rows)
    margin = jnp.zeros((rows, MAXLAG), jnp.bfloat16)
    blocks = [every_ref[chan_at, at, pl.ds(start, rows), :] for at in range(time_count)]
    own = jnp.concatenate([margin] + blocks + [margin], axis=1).astype(jnp.float32)
    if rows != row_share:
        own = pltpu.roll(own, rows - lax.rem(row_at, rows), 0)
    tail = jnp.zeros((group_ch, MAXLAG), jnp.bfloat16)
    weights = []
    for match in range(match_count):
        partner = matchings_ref[match, chan_at]
        blocks = [every_ref[partner, at] for at in range(time_count)]
        ahead = jnp.concatenate(blocks + [tail], axis=1)
        behind = pltpu.roll(ahead.astype(jnp.float32), 1, 1).astype(jnp.bfloat16)
        weights += [behind, ahead]
    weights = jnp.concatenate(weights, axis=0)
    pair = 2 * group_ch
    per_chunk = 16
    for first in range(0, LAGS, 2 * per_chunk):
        lags = range(first, min(first + 2 * per_chunk, LAGS), 2)
        lagged = jnp.concatenate(
            [
                pltpu.roll(own, (lag - (2 * MAXLAG - 1)) % width, 1)[:, :depth].astype(jnp.bfloat16)
                for lag in lags
            ],
            axis=0,
        )
        summed = lax.dot_general(
            lagged, weights, (((1,), (1,)), ((), ())), preferred_element_type=jnp.float32
        )
        scaled = (summed * scaling).astype(jnp.bfloat16)
        for at, lag in enumerate(lags):
            span = min(pair, (LAGS - lag) * group_ch)
            for match in range(match_count):
                out_ref[match, 0, :, lag * group_ch : lag * group_ch + span] = scaled[
                    at * rows : at * rows + row_share, match * pair : match * pair + span
                ]


def local(records, fir_taps, matchings):
    group_ch, samples_dev = records.shape
    group_count, time_count = lax.axis_size("chan"), lax.axis_size("tm")
    match_count = matchings.shape[0]
    width = samples_dev + 2 * HALO
    chips = group_count // CORES
    sends = time_count - 1 + time_count * (2 * chips - 1)
    every = pl.pallas_call(
        functools.partial(gather, time_count, group_count),
        out_shape=jax.ShapeDtypeStruct(
            (group_count, time_count, group_ch, samples_dev), jnp.bfloat16
        ),
        in_specs=[pl.BlockSpec(memory_space=pltpu.VMEM)] * 2,
        out_specs=pl.BlockSpec(memory_space=pltpu.VMEM),
        scratch_shapes=[
            pltpu.VMEM((group_ch, width), jnp.float32),
            pltpu.VMEM((8, width), jnp.float32),
            pltpu.SemaphoreType.DMA((2,)),
            pltpu.SemaphoreType.DMA((2,)),
            pltpu.SemaphoreType.DMA((sends,)),
            pltpu.SemaphoreType.DMA((group_count, time_count)),
        ],
        compiler_params=pltpu.CompilerParams(collective_id=0, has_side_effects=True),
    )(records, fir_taps.reshape(1, -1))
    row_share = group_ch // time_count
    scaling = 1.0 / math.sqrt(samples_dev * time_count)
    return pl.pallas_call(
        functools.partial(correlate, row_share, scaling),
        out_shape=jax.ShapeDtypeStruct(
            (match_count, 1, row_share, LAGS * group_ch), jnp.bfloat16
        ),
        in_specs=[
            pl.BlockSpec(memory_space=pltpu.SMEM),
            pl.BlockSpec(memory_space=pltpu.VMEM),
        ],
        out_specs=pl.BlockSpec(memory_space=pltpu.VMEM),
    )(matchings, every)


def solution(mesh):
    in_specs = (P(("parts", "chan"), "tm"), P(), P())
    out_specs = P(None, ("parts", "chan"), "tm", None)
    return jax.shard_map(local, mesh=mesh, in_specs=in_specs, out_specs=out_specs, check_vma=False)
```

time: 43.2 us -> 24.6 us (0.57)
  blocking collectives: 20.9 us -> 0 us
  Pallas kernels: 3.73 us -> 24.4 us
  starting transfers between devices: 11.1 us -> 0 us
  local copies, waits for them, and re-layouts: 3.54 us -> 0 us
  other arithmetic: 1.91 us -> 0 us
  matrix products: 1.59 us -> 0 us
    all_gather x2 -> x0, blocking collectives: 20.9 us -> none  [the longest x1 15.2 us: local(): incoming = lax.all_gather(partners, 'tm', axis=2, tiled=True)]
    pallas_call x0 -> x1, Pallas kernels: none -> 20.6 us  [local(): pl.pallas_call(functools.partial(gather, time_count, group_count), out_sh...]
    ppermute x2 -> x0, starting transfers between devices: 6.87 us -> none  [the longest x1 5.59 us: extended_2(): lax.ppermute(tail, axis, [(i, (i + 1) % count) for i in range(ends)])]
    all_to_all x1 -> x0, starting transfers between devices: 4.24 us -> none  [local(): lax.all_to_all(normed, 'tm', split_axis=0, concat_axis=1, tiled=True)]
    dot_general x2 -> x0, matrix products: 1.59 us -> none  [the longest x1 0.88 us: normalize(): jnp.dot(magnitude, band_matrix, precision=lax.Precision.HIGHEST, preferre...]
    reshape x2 -> x0, local copies, waits for them, and re-layouts: 1.43 us -> none  [the longest x1 1.34 us: falling(): repeated.reshape(leading + (row_count, span_width - 1))[..., row_count - 1:]]
    select_n x2 -> x0, other arithmetic: 0.95 us -> none  [local(): partners = jnp.take(every_group, matchings[:, group_index], axis=0)]
    slice x1 -> x0, local copies, waits for them, and re-layouts: 0.85 us -> none  [extended_2(): lax.slice_in_dim(cells, cells.shape[dim] - width, cells.shape[dim], axis=...]
  transfers between devices with their start and end apart: 3 -> 0, of which waited for: 0 -> 0; matrix products, arithmetic and copies ran while one was open for 9% -> 0% of each run, Pallas kernels for 0% -> 0%
where the time goes in v2:
time: 24.6 us; the launch traced here: 24.4 us
  Pallas kernels  24.4 us (99%)
    pallas_call x1, Pallas kernels, local(): pl.pallas_call(functools.partial(gather, time_count, group_count), out_sh...  20.6 us
    pallas_call x1, Pallas kernels, local(): pl.pallas_call(functools.partial(correlate, row_share, scaling), out_shap...  3.82 us

profile of v2, /device:TPU:0, one launch (start us, length us, event | category | flops | bytes accessed | tf_op | source)
XLA Modules:
  0.0 24.4 jit_solution(12285160474420868343)
XLA Ops:
  0.0 20.6 %shard_map.37.every_ref = bf16[4,4,64,256]{3,2,1,0:T(8,128)(2,1)} custom-call(f32[64,256]{1,0:T(8,128)} %records_ref.1, f32[1,129]{1,0:T(1,128)} %bitcast.1), custom_call_target="tpu_custom_call" | custom-call | tf_op jit(solution)/shard_map/pallas_call | solution.py:229
  20.6 3.8 %shard_map.38 = bf16[2,1,16,16448]{3,2,1,0:T(8,128)(2,1)} custom-call(s32[2,4]{1,0:T(2,128)} %matchings_ref.1, bf16[4,4,64,256]{3,2,1,0:T(8,128)(2,1)} %shard_map.37.every_ref), custom_call_target="tpu_custom_call" | custom-call | tf_op jit(solution)/shard_map/pallas_call | solution.py:248

commit v3 on v2

--- a/solution.py
+++ b/solution.py
@@ -21,17 +21,6 @@
     high = values.astype(jnp.bfloat16)
     low = (values - high.astype(jnp.float32)).astype(jnp.bfloat16)
     return high, low
-
-
-def flipped(at, step, count):
-    if count & (count - 1):
-        return lax.rem(at + step, count)
-    bit = 1
-    while bit <= step:
-        if step & bit:
-            at = at + bit * (1 - 2 * lax.rem(at // bit, 2))
-        bit *= 2
-    return at
 
 
 def gather(
@@ -53,13 +42,20 @@
     chips = group_count // CORES
     chip_at, core_at = chan_at // CORES, lax.rem(chan_at, CORES)
     sibling = {"chan": chan_at + 1 - 2 * core_at}
-    times = [flipped(time_at, step, time_count) for step in range(time_count)]
+    times = [time_at] + [
+        step + (step >= time_at).astype(jnp.int32) for step in range(time_count - 1)
+    ]
+    has_next, has_last = time_at < time_count - 1, time_at > 0
     others = [
         lax.rem(chip_at + step, chips) * CORES + core_at for step in range(1, chips)
     ]
 
     barrier = pltpu.get_barrier_semaphore()
-    peers = [{"tm": at} for at in times[1:]] + [{"chan": at} for at in others] + [sibling]
+    peers = [{"chan": at} for at in others] + [sibling]
+    for present, at in ((has_next, time_at + 1), (has_last, time_at - 1)):
+        pl.when(present)(
+            functools.partial(pl.semaphore_signal, barrier, inc=1, device_id={"tm": at})
+        )
     for peer in peers:
         pl.semaphore_signal(barrier, inc=1, device_id=peer)
 
@@ -74,7 +70,9 @@
         stride_axis=0,
     )
     fir_high, fir_low = split(fir)
-    pl.semaphore_wait(barrier, len(peers))
+    pl.semaphore_wait(
+        barrier, len(peers) + has_next.astype(jnp.int32) + has_last.astype(jnp.int32)
+    )
 
     def halo(source, target, side, to):
         return pltpu.make_async_remote_copy(
@@ -87,7 +85,6 @@
 
     to_next = halo(pl.ds(samples - HALO, HALO), pl.ds(0, HALO), 0, time_at + 1)
     to_last = halo(pl.ds(0, HALO), pl.ds(samples + HALO, HALO), 1, time_at - 1)
-    has_next, has_last = time_at < time_count - 1, time_at > 0
     pl.when(has_next)(to_next.start)
     pl.when(has_last)(to_last.start)
     wide[:, HALO : HALO + samples] = records_ref[...]
@@ -126,7 +123,7 @@
 
     sent = []
 
-    def push(chan_from, time_from, to):
+    def push(chan_from, time_from, to, wanted=None):
         block = every_ref.at[chan_from, time_from]
         copy = pltpu.make_async_remote_copy(
             src_ref=block,
@@ -135,8 +132,19 @@
             recv_sem=recv_sem.at[chan_from, time_from],
             device_id=to,
         )
-        copy.start()
-        sent.append(copy)
+        sent.append((wanted, copy))
+        if wanted is None:
+            copy.start()
+        else:
+            pl.when(wanted)(copy.start)
+
+    def onward(time_from):
+        even = lax.rem(jnp.abs(time_at - time_from), 2) == 0
+        for hop in (2, 1):
+            up = even & (time_from <= time_at) & (time_at + hop < time_count)
+            push(chan_at, time_from, {"tm": time_at + hop}, up)
+            down = even & (time_from >= time_at) & (time_at >= hop)
+            push(chan_at, time_from, {"tm": time_at - hop}, down)
 
     def arrived(chan_from, time_from):
         block = every_ref.at[chan_from, time_from]
@@ -148,11 +156,10 @@
             device_id=sibling,
         ).wait_recv()
 
-    for time_to in reversed(times[1:]):
-        push(chan_at, time_at, {"tm": time_to})
     for step, time_from in enumerate(times):
         if step:
             arrived(chan_at, time_from)
+        onward(time_from)
         for chan_to in others:
             push(chan_at, time_from, {"chan": chan_to})
         push(chan_at, time_from, sibling)
@@ -166,8 +173,11 @@
     for time_from in times:
         for chan_from in [chan_at] + others:
             arrived(chan_from + 1 - 2 * core_at, time_from)
-    for copy in sent:
-        copy.wait_send()
+    for wanted, copy in sent:
+        if wanted is None:
+            copy.wait_send()
+        else:
+            pl.when(wanted)(copy.wait_send)
     pl.when(has_next)(to_next.wait_send)
     pl.when(has_last)(to_last.wait_send)
 
@@ -225,7 +235,7 @@
     match_count = matchings.shape[0]
     width = samples_dev + 2 * HALO
     chips = group_count // CORES
-    sends = time_count - 1 + time_count * (2 * chips - 1)
+    sends = time_count * (2 * chips + 3)
     every = pl.pallas_call(
         functools.partial(gather, time_count, group_count),
         out_shape=jax.ShapeDtypeStruct(

time: 24.6 us -> 26.1 us (1.061)
  Pallas kernels: 24.4 us -> 26 us
    pallas_call x1, Pallas kernels: 20.6 us -> 22.1 us  [local(): pl.pallas_call(functools.partial(gather, time_count, group_count), out_sh...]
where the time goes in v3:
time: 26.1 us; the launch traced here: 26 us
  Pallas kernels  26 us (100%)
    pallas_call x1, Pallas kernels, local(): pl.pallas_call(functools.partial(gather, time_count, group_count), out_sh...  22.1 us
    pallas_call x1, Pallas kernels, local(): pl.pallas_call(functools.partial(correlate, row_share, scaling), out_shap...  3.82 us

profile of v3, /device:TPU:0, one launch (start us, length us, event | category | flops | bytes accessed | tf_op | source)
XLA Modules:
  0.0 26.0 jit_solution(10327369417676217303)
XLA Ops:
  0.0 22.1 %shard_map.37.every_ref = bf16[4,4,64,256]{3,2,1,0:T(8,128)(2,1)} custom-call(f32[64,256]{1,0:T(8,128)} %records_ref.1, f32[1,129]{1,0:T(1,128)} %bitcast.1), custom_call_target="tpu_custom_call" | custom-call | tf_op jit(solution)/shard_map/pallas_call | solution.py:239
  22.1 3.8 %shard_map.38 = bf16[2,1,16,16448]{3,2,1,0:T(8,128)(2,1)} custom-call(s32[2,4]{1,0:T(2,128)} %matchings_ref.1, bf16[4,4,64,256]{3,2,1,0:T(8,128)(2,1)} %shard_map.37.every_ref), custom_call_target="tpu_custom_call" | custom-call | tf_op jit(solution)/shard_map/pallas_call | solution.py:258

commit v4 on v2

--- a/solution.py
+++ b/solution.py
@@ -59,7 +59,8 @@
     ]
 
     barrier = pltpu.get_barrier_semaphore()
-    peers = [{"tm": at} for at in times[1:]] + [{"chan": at} for at in others] + [sibling]
+    cross = [at + 1 - 2 * core_at for at in others]
+    peers = [{"tm": at} for at in times[1:]] + [{"chan": at} for at in others + cross] + [sibling]
     for peer in peers:
         pl.semaphore_signal(barrier, inc=1, device_id=peer)
 
@@ -153,19 +154,13 @@
     for step, time_from in enumerate(times):
         if step:
             arrived(chan_at, time_from)
-        for chan_to in others:
+        for chan_to in others + cross:
             push(chan_at, time_from, {"chan": chan_to})
         push(chan_at, time_from, sibling)
-        if step:
-            for chan_from in others:
-                arrived(chan_from, times[step - 1])
-                push(chan_from, times[step - 1], sibling)
-    for chan_from in others:
-        arrived(chan_from, times[-1])
-        push(chan_from, times[-1], sibling)
     for time_from in times:
-        for chan_from in [chan_at] + others:
-            arrived(chan_from + 1 - 2 * core_at, time_from)
+        for chan_from in others + cross:
+            arrived(chan_from, time_from)
+        arrived(chan_at + 1 - 2 * core_at, time_from)
     for copy in sent:
         copy.wait_send()
     pl.when(has_next)(to_next.wait_send)
@@ -225,7 +220,7 @@
     match_count = matchings.shape[0]
     width = samples_dev + 2 * HALO
     chips = group_count // CORES
-    sends = time_count - 1 + time_count * (2 * chips - 1)
+    sends = time_count - 1 + time_count * (4 * chips)
     every = pl.pallas_call(
         functools.partial(gather, time_count, group_count),
         out_shape=jax.ShapeDtypeStruct(

time: 24.6 us -> 22.6 us (0.919)
  Pallas kernels: 24.4 us -> 22.5 us
    pallas_call x1, Pallas kernels: 20.6 us -> 18.6 us  [local(): pl.pallas_call(functools.partial(gather, time_count, group_count), out_sh...]
where the time goes in v4:
time: 22.6 us; the launch traced here: 22.5 us
  Pallas kernels  22.5 us (100%)
    pallas_call x1, Pallas kernels, local(): pl.pallas_call(functools.partial(gather, time_count, group_count), out_sh...  18.6 us
    pallas_call x1, Pallas kernels, local(): pl.pallas_call(functools.partial(correlate, row_share, scaling), out_shap...  3.82 us

profile of v4, /device:TPU:0, one launch (start us, length us, event | category | flops | bytes accessed | tf_op | source)
XLA Modules:
  0.0 22.5 jit_solution(8868712505319636358)
XLA Ops:
  0.0 18.6 %shard_map.37.every_ref = bf16[4,4,64,256]{3,2,1,0:T(8,128)(2,1)} custom-call(f32[64,256]{1,0:T(8,128)} %records_ref.1, f32[1,129]{1,0:T(1,128)} %bitcast.1), custom_call_target="tpu_custom_call" | custom-call | tf_op jit(solution)/shard_map/pallas_call | solution.py:224
  18.6 3.8 %shard_map.38 = bf16[2,1,16,16448]{3,2,1,0:T(8,128)(2,1)} custom-call(s32[2,4]{1,0:T(2,128)} %matchings_ref.1, bf16[4,4,64,256]{3,2,1,0:T(8,128)(2,1)} %shard_map.37.every_ref), custom_call_target="tpu_custom_call" | custom-call | tf_op jit(solution)/shard_map/pallas_call | solution.py:243

commit v5 on v4

v5 whole, which is shorter than its diff:
```python
import functools
import math

import jax
import jax.numpy as jnp
from jax import lax
from jax.experimental import pallas as pl
from jax.experimental.pallas import tpu as pltpu
from jax.sharding import PartitionSpec as P

AVG = 65
MAXLAG = 128
LAGS = 257
HALO = 128
CORES = 2

EPSILON = 1e-05


def split(values):
    high = values.astype(jnp.bfloat16)
    low = (values - high.astype(jnp.float32)).astype(jnp.bfloat16)
    return high, low


def flipped(at, step, count):
    if count & (count - 1):
        return lax.rem(at + step, count)
    bit = 1
    while bit <= step:
        if step & bit:
            at = at + bit * (1 - 2 * lax.rem(at // bit, 2))
        bit *= 2
    return at


def gather(
    time_count,
    group_count,
    records_ref,
    every_ref,
    send_sem,
    recv_sem,
):
    time_at, chan_at = lax.axis_index("tm"), lax.axis_index("chan")
    chips = group_count // CORES
    chip_at, core_at = chan_at // CORES, lax.rem(chan_at, CORES)
    sibling = {"chan": chan_at + 1 - 2 * core_at}
    times = [flipped(time_at, step, time_count) for step in range(time_count)]
    others = [
        lax.rem(chip_at + step, chips) * CORES + core_at for step in range(1, chips)
    ]

    barrier = pltpu.get_barrier_semaphore()
    cross = [at + 1 - 2 * core_at for at in others]
    peers = [{"tm": at} for at in times[1:]] + [{"chan": at} for at in others + cross] + [sibling]
    for peer in peers:
        pl.semaphore_signal(barrier, inc=1, device_id=peer)

    every_ref[chan_at, time_at] = records_ref[...].astype(jnp.bfloat16)
    pl.semaphore_wait(barrier, len(peers))

    sent = []

    def push(chan_from, time_from, to):
        block = every_ref.at[chan_from, time_from]
        copy = pltpu.make_async_remote_copy(
            src_ref=block,
            dst_ref=block,
            send_sem=send_sem.at[len(sent)],
            recv_sem=recv_sem.at[chan_from, time_from],
            device_id=to,
        )
        copy.start()
        sent.append(copy)

    def arrived(chan_from, time_from):
        block = every_ref.at[chan_from, time_from]
        pltpu.make_async_remote_copy(
            src_ref=block,
            dst_ref=block,
            send_sem=send_sem.at[0],
            recv_sem=recv_sem.at[chan_from, time_from],
            device_id=sibling,
        ).wait_recv()

    for time_to in reversed(times[1:]):
        push(chan_at, time_at, {"tm": time_to})
    for step, time_from in enumerate(times):
        if step:
            arrived(chan_at, time_from)
        for chan_to in others + cross:
            push(chan_at, time_from, {"chan": chan_to})
        push(chan_at, time_from, sibling)
    for time_from in times:
        for chan_from in others + cross:
            arrived(chan_from, time_from)
        arrived(chan_at + 1 - 2 * core_at, time_from)
    for copy in sent:
        copy.wait_send()


def normalize(values, taps_ref, taps_row, block):
    rows, samples = values.shape
    width = block + 2 * HALO
    starts = range(0, samples, block)
    taps_row[...] = jnp.zeros_like(taps_row)
    taps_row[0:1, 0 : taps_ref.shape[1]] = taps_ref[...]
    fir = pltpu.roll(
        jnp.broadcast_to(taps_row[0:1, :], (width, width)),
        width - taps_ref.shape[1] // 2,
        1,
        stride=1,
        stride_axis=0,
    )[:, HALO : HALO + block]
    rows_at = lax.broadcasted_iota(jnp.int32, (width, block), 0)
    cols_at = lax.broadcasted_iota(jnp.int32, (width, block), 1) + HALO
    band = (jnp.abs(rows_at - cols_at) <= AVG // 2).astype(jnp.float32).astype(jnp.bfloat16)

    def spans(values):
        margin = jnp.zeros((rows, HALO), values.dtype)
        padded = jnp.concatenate([margin, values, margin], axis=1)
        return jnp.concatenate([padded[:, at : at + width] for at in starts], axis=0)

    def dot(left, right):
        return jnp.dot(left, right, preferred_element_type=jnp.float32)

    fir_high, fir_low = split(fir)
    wide = spans(values)
    filtered = dot(wide, fir_high) + dot(wide, fir_low)
    merged = jnp.concatenate(
        [filtered[at : at + rows] for at in range(0, rows * len(starts), rows)], axis=1
    )
    high, low = split(jnp.abs(merged))
    summed = dot(spans(high), band) + dot(spans(low), band)
    normed = (filtered / (summed / AVG + EPSILON)).astype(jnp.bfloat16)
    return jnp.concatenate(
        [normed[at : at + rows] for at in range(0, rows * len(starts), rows)], axis=1
    )


def correlate(row_share, scaling, matchings_ref, taps_ref, every_ref, out_ref, taps_row):
    _, time_count, group_ch, samples_dev = every_ref.shape
    match_count = matchings_ref.shape[0]
    samples = time_count * samples_dev
    chan_at, time_at = lax.axis_index("chan"), lax.axis_index("tm")
    depth = samples + MAXLAG
    width = samples + 2 * MAXLAG
    rows = -(-row_share // 16) * 16
    row_at = time_at * row_share
    start = pl.multiple_of(row_at // rows * rows, rows)
    picked = [[every_ref[chan_at, at, pl.ds(start, rows), :] for at in range(time_count)]]
    for match in range(match_count):
        partner = matchings_ref[match, chan_at]
        picked.append([every_ref[partner, at] for at in range(time_count)])
    picked = jnp.concatenate([jnp.concatenate(blocks, axis=1) for blocks in picked], axis=0)
    normed = normalize(picked, taps_ref, taps_row, samples_dev)
    margin = jnp.zeros((rows, MAXLAG), jnp.bfloat16)
    own = jnp.concatenate([margin, normed[0:rows], margin], axis=1).astype(jnp.float32)
    if rows != row_share:
        own = pltpu.roll(own, rows - lax.rem(row_at, rows), 0)
    tail = jnp.zeros((group_ch, MAXLAG), jnp.bfloat16)
    weights = []
    for match in range(match_count):
        at = rows + match * group_ch
        ahead = jnp.concatenate([normed[at : at + group_ch], tail], axis=1)
        behind = pltpu.roll(ahead.astype(jnp.float32), 1, 1).astype(jnp.bfloat16)
        weights += [behind, ahead]
    weights = jnp.concatenate(weights, axis=0)
    pair = 2 * group_ch
    per_chunk = 16
    for first in range(0, LAGS, 2 * per_chunk):
        lags = range(first, min(first + 2 * per_chunk, LAGS), 2)
        lagged = jnp.concatenate(
            [
                pltpu.roll(own, (lag - (2 * MAXLAG - 1)) % width, 1)[:, :depth].astype(jnp.bfloat16)
                for lag in lags
            ],
            axis=0,
        )
        summed = lax.dot_general(
            lagged, weights, (((1,), (1,)), ((), ())), preferred_element_type=jnp.float32
        )
        scaled = (summed * scaling).astype(jnp.bfloat16)
        for at, lag in enumerate(lags):
            span = min(pair, (LAGS - lag) * group_ch)
            for match in range(match_count):
                out_ref[match, 0, :, lag * group_ch : lag * group_ch + span] = scaled[
                    at * rows : at * rows + row_share, match * pair : match * pair + span
                ]


def local(records, fir_taps, matchings):
    group_ch, samples_dev = records.shape
    group_count, time_count = lax.axis_size("chan"), lax.axis_size("tm")
    match_count = matchings.shape[0]
    chips = group_count // CORES
    sends = time_count - 1 + time_count * (4 * chips)
    every = pl.pallas_call(
        functools.partial(gather, time_count, group_count),
        out_shape=jax.ShapeDtypeStruct(
            (group_count, time_count, group_ch, samples_dev), jnp.bfloat16
        ),
        in_specs=[pl.BlockSpec(memory_space=pltpu.VMEM)],
        out_specs=pl.BlockSpec(memory_space=pltpu.VMEM),
        scratch_shapes=[
            pltpu.SemaphoreType.DMA((sends,)),
            pltpu.SemaphoreType.DMA((group_count, time_count)),
        ],
        compiler_params=pltpu.CompilerParams(collective_id=0, has_side_effects=True),
    )(records)
    row_share = group_ch // time_count
    scaling = 1.0 / math.sqrt(samples_dev * time_count)
    return pl.pallas_call(
        functools.partial(correlate, row_share, scaling),
        out_shape=jax.ShapeDtypeStruct(
            (match_count, 1, row_share, LAGS * group_ch), jnp.bfloat16
        ),
        in_specs=[
            pl.BlockSpec(memory_space=pltpu.SMEM),
            pl.BlockSpec(memory_space=pltpu.VMEM),
            pl.BlockSpec(memory_space=pltpu.VMEM),
        ],
        out_specs=pl.BlockSpec(memory_space=pltpu.VMEM),
        scratch_shapes=[pltpu.VMEM((8, samples_dev + 2 * HALO), jnp.float32)],
    )(matchings, fir_taps.reshape(1, -1), every)


def solution(mesh):
    in_specs = (P(("parts", "chan"), "tm"), P(), P())
    out_specs = P(None, ("parts", "chan"), "tm", None)
    return jax.shard_map(local, mesh=mesh, in_specs=in_specs, out_specs=out_specs, check_vma=False)
```

time: 22.6 us -> 20.9 us (0.925)
  Pallas kernels: 22.5 us -> 20.7 us
    pallas_call x1, Pallas kernels: 18.6 us -> 15.6 us  [local(): pl.pallas_call(functools.partial(gather, time_count, group_count), out_sh...]
    pallas_call x1, Pallas kernels: 3.82 us -> 5.1 us  [local(): pl.pallas_call(functools.partial(correlate, row_share, scaling), out_shap...]
where the time goes in v5:
time: 20.9 us; the launch traced here: 20.7 us
  Pallas kernels  20.7 us (99%)
    pallas_call x1, Pallas kernels, local(): pl.pallas_call(functools.partial(gather, time_count, group_count), out_sh...  15.6 us
    pallas_call x1, Pallas kernels, local(): pl.pallas_call(functools.partial(correlate, row_share, scaling), out_shap...  5.1 us

profile of v5, /device:TPU:0, one launch (start us, length us, event | category | flops | bytes accessed | tf_op | source)
XLA Modules:
  0.0 20.7 jit_solution(13565042994691568065)
XLA Ops:
  0.0 15.6 %shard_map.37.every_ref = bf16[4,4,64,256]{3,2,1,0:T(8,128)(2,1)} custom-call(f32[64,256]{1,0:T(8,128)} %records_ref.1), custom_call_target="tpu_custom_call" | custom-call | tf_op jit(solution)/shard_map/pallas_call | solution.py:199
  15.6 5.1 %shard_map.38 = bf16[2,1,16,16448]{3,2,1,0:T(8,128)(2,1)} custom-call(s32[2,4]{1,0:T(2,128)} %matchings_ref.1, f32[1,129]{1,0:T(1,128)} %bitcast.1, bf16[4,4,64,256]{3,2,1,0:T(8,128)(2,1)} %shard_map.37.every_ref), custom_call_target="tpu_custom_call" | custom-call | tf_op jit(solution)/shard_map/pallas_call | solution.py:214

commit v6 on v5

v6 whole, which is shorter than its diff:
```python
import functools
import math

import jax
import jax.numpy as jnp
from jax import lax
from jax.experimental import pallas as pl
from jax.experimental.pallas import tpu as pltpu
from jax.sharding import PartitionSpec as P

AVG = 65
MAXLAG = 128
LAGS = 257
HALO = 128
CORES = 2

EPSILON = 1e-05


def split(values):
    high = values.astype(jnp.bfloat16)
    low = (values - high.astype(jnp.float32)).astype(jnp.bfloat16)
    return high, low


def flipped(at, step, count):
    if count & (count - 1):
        return lax.rem(at + step, count)
    bit = 1
    while bit <= step:
        if step & bit:
            at = at + bit * (1 - 2 * lax.rem(at // bit, 2))
        bit *= 2
    return at


def prepare(taps_ref, taps_row, block):
    width = block + 2 * HALO
    taps_row[...] = jnp.zeros_like(taps_row)
    taps_row[0:1, 0 : taps_ref.shape[1]] = taps_ref[...]
    fir = pltpu.roll(
        jnp.broadcast_to(taps_row[0:1, :], (width, width)),
        width - taps_ref.shape[1] // 2,
        1,
        stride=1,
        stride_axis=0,
    )[:, HALO : HALO + block]
    rows_at = lax.broadcasted_iota(jnp.int32, (width, block), 0)
    cols_at = lax.broadcasted_iota(jnp.int32, (width, block), 1) + HALO
    band = (jnp.abs(rows_at - cols_at) <= AVG // 2).astype(jnp.float32).astype(jnp.bfloat16)
    return split(fir) + (band,)


def normalize(values, prepared, block):
    fir_high, fir_low, band = prepared
    rows, samples = values.shape
    width = block + 2 * HALO
    starts = range(0, samples, block)

    def spans(values):
        margin = jnp.zeros((rows, HALO), values.dtype)
        padded = jnp.concatenate([margin, values, margin], axis=1)
        return jnp.concatenate([padded[:, at : at + width] for at in starts], axis=0)

    def dot(left, right):
        return jnp.dot(left, right, preferred_element_type=jnp.float32)

    wide = spans(values)
    filtered = dot(wide, fir_high) + dot(wide, fir_low)
    merged = jnp.concatenate(
        [filtered[at : at + rows] for at in range(0, rows * len(starts), rows)], axis=1
    )
    high, low = split(jnp.abs(merged))
    summed = dot(spans(high), band) + dot(spans(low), band)
    normed = (filtered / (summed / AVG + EPSILON)).astype(jnp.bfloat16)
    return jnp.concatenate(
        [normed[at : at + rows] for at in range(0, rows * len(starts), rows)], axis=1
    )


def gather(
    time_count,
    group_count,
    row_share,
    scaling,
    matchings_hbm,
    taps_hbm,
    records_hbm,
    out_ref,
    matchings_ref,
    taps_ref,
    records_ref,
    load_sem,
    every_ref,
    lagged_ref,
    taps_row,
    send_sem,
    recv_sem,
):
    time_at, chan_at = lax.axis_index("tm"), lax.axis_index("chan")
    chips = group_count // CORES
    chip_at, core_at = chan_at // CORES, lax.rem(chan_at, CORES)
    sibling = {"chan": chan_at + 1 - 2 * core_at}
    times = [flipped(time_at, step, time_count) for step in range(time_count)]
    others = [
        lax.rem(chip_at + step, chips) * CORES + core_at for step in range(1, chips)
    ]

    barrier = pltpu.get_barrier_semaphore()
    cross = [at + 1 - 2 * core_at for at in others]
    peers = [{"tm": at} for at in times[1:]] + [{"chan": at} for at in others + cross] + [sibling]
    for peer in peers:
        pl.semaphore_signal(barrier, inc=1, device_id=peer)

    loads = [
        pltpu.make_async_copy(source, target, load_sem.at[at])
        for at, (source, target) in enumerate(
            (
                (records_hbm, records_ref),
                (taps_hbm, taps_ref),
                (matchings_hbm, matchings_ref),
            )
        )
    ]
    for load in loads:
        load.start()
    for load in loads:
        load.wait()
    every_ref[chan_at, time_at] = records_ref[...].astype(jnp.bfloat16)
    pl.semaphore_wait(barrier, len(peers))

    sent = []

    def push(chan_from, time_from, to):
        block = every_ref.at[chan_from, time_from]
        copy = pltpu.make_async_remote_copy(
            src_ref=block,
            dst_ref=block,
            send_sem=send_sem.at[len(sent)],
            recv_sem=recv_sem.at[chan_from, time_from],
            device_id=to,
        )
        copy.start()
        sent.append(copy)

    def arrived(chan_from, time_from):
        block = every_ref.at[chan_from, time_from]
        pltpu.make_async_remote_copy(
            src_ref=block,
            dst_ref=block,
            send_sem=send_sem.at[0],
            recv_sem=recv_sem.at[chan_from, time_from],
            device_id=sibling,
        ).wait_recv()

    for time_to in reversed(times[1:]):
        push(chan_at, time_at, {"tm": time_to})
    for step, time_from in enumerate(times):
        if step:
            arrived(chan_at, time_from)
        for chan_to in others + cross:
            push(chan_at, time_from, {"chan": chan_to})
        push(chan_at, time_from, sibling)
    samples_dev = every_ref.shape[3]
    group_ch, match_count = every_ref.shape[2], matchings_ref.shape[0]
    samples = time_count * samples_dev
    depth, width = samples + MAXLAG, samples + 2 * MAXLAG
    rows = -(-row_share // 16) * 16
    row_at = time_at * row_share
    start = pl.multiple_of(row_at // rows * rows, rows)
    prepared = prepare(taps_ref, taps_row, samples_dev)
    own = jnp.concatenate(
        [every_ref[chan_at, at, pl.ds(start, rows), :] for at in range(time_count)], axis=1
    )
    own = normalize(own, prepared, samples_dev)
    margin = jnp.zeros((rows, MAXLAG), jnp.bfloat16)
    own = jnp.concatenate([margin, own, margin], axis=1).astype(jnp.float32)
    if rows != row_share:
        own = pltpu.roll(own, rows - lax.rem(row_at, rows), 0)
    for lag in range(0, LAGS, 2):
        shifted = pltpu.roll(own, (lag - (2 * MAXLAG - 1)) % width, 1)[:, :depth]
        lagged_ref[lag // 2 * rows : (lag // 2 + 1) * rows, :] = shifted.astype(jnp.bfloat16)
    for time_from in times:
        for chan_from in others + cross:
            arrived(chan_from, time_from)
        arrived(chan_at + 1 - 2 * core_at, time_from)
    picked = []
    for match in range(match_count):
        partner = matchings_ref[match, chan_at]
        picked.append(
            jnp.concatenate([every_ref[partner, at] for at in range(time_count)], axis=1)
        )
    normed = normalize(jnp.concatenate(picked, axis=0), prepared, samples_dev)
    tail = jnp.zeros((group_ch, MAXLAG), jnp.bfloat16)
    weights = []
    for match in range(match_count):
        at = match * group_ch
        ahead = jnp.concatenate([normed[at : at + group_ch], tail], axis=1)
        behind = pltpu.roll(ahead.astype(jnp.float32), 1, 1).astype(jnp.bfloat16)
        weights += [behind, ahead]
    weights = jnp.concatenate(weights, axis=0)
    pair = 2 * group_ch
    per_chunk = 16
    for first in range(0, LAGS, 2 * per_chunk):
        lags = range(first, min(first + 2 * per_chunk, LAGS), 2)
        lagged = lagged_ref[first // 2 * rows : (first // 2 + len(lags)) * rows, :]
        summed = lax.dot_general(
            lagged, weights, (((1,), (1,)), ((), ())), preferred_element_type=jnp.float32
        )
        scaled = (summed * scaling).astype(jnp.bfloat16)
        for at, lag in enumerate(lags):
            span = min(pair, (LAGS - lag) * group_ch)
            for match in range(match_count):
                out_ref[match, 0, :, lag * group_ch : lag * group_ch + span] = scaled[
                    at * rows : at * rows + row_share, match * pair : match * pair + span
                ]
    for copy in sent:
        copy.wait_send()


def local(records, fir_taps, matchings):
    group_ch, samples_dev = records.shape
    group_count, time_count = lax.axis_size("chan"), lax.axis_size("tm")
    match_count = matchings.shape[0]
    chips = group_count // CORES
    sends = time_count - 1 + time_count * (4 * chips)
    samples = samples_dev * time_count
    row_share = group_ch // time_count
    rows = -(-row_share // 16) * 16
    scaling = 1.0 / math.sqrt(samples)
    return pl.pallas_call(
        functools.partial(gather, time_count, group_count, row_share, scaling),
        out_shape=jax.ShapeDtypeStruct(
            (match_count, 1, row_share, LAGS * group_ch), jnp.bfloat16
        ),
        in_specs=[pl.BlockSpec(memory_space=pltpu.HBM)] * 3,
        out_specs=pl.BlockSpec(memory_space=pltpu.VMEM),
        scratch_shapes=[
            pltpu.SMEM(matchings.shape, jnp.int32),
            pltpu.VMEM((1,) + fir_taps.shape, jnp.float32),
            pltpu.VMEM(records.shape, jnp.float32),
            pltpu.SemaphoreType.DMA((3,)),
            pltpu.VMEM((group_count, time_count, group_ch, samples_dev), jnp.bfloat16),
            pltpu.VMEM(((LAGS + 1) // 2 * rows, samples + MAXLAG), jnp.bfloat16),
            pltpu.VMEM((8, samples_dev + 2 * HALO), jnp.float32),
            pltpu.SemaphoreType.DMA((sends,)),
            pltpu.SemaphoreType.DMA((group_count, time_count)),
        ],
        compiler_params=pltpu.CompilerParams(vmem_limit_bytes=40<<20, collective_id=0, has_side_effects=True),
    )(matchings, fir_taps.reshape(1, -1), records)


def solution(mesh):
    in_specs = (P(("parts", "chan"), "tm"), P(), P())
    out_specs = P(None, ("parts", "chan"), "tm", None)
    return jax.shard_map(local, mesh=mesh, in_specs=in_specs, out_specs=out_specs, check_vma=False)
```

time: 20.9 us -> 20.1 us (0.962)
  Pallas kernels: 20.7 us -> 16.7 us
  local copies, waits for them, and re-layouts: 0 us -> 3.17 us
    pallas_call x2 -> x1, Pallas kernels: 20.7 us -> 16.7 us  [local(): pl.pallas_call(functools.partial(gather, time_count, group_count, row_sha...]
    unnamed x0 -> x7, local copies, waits for them, and re-layouts: none -> 3.17 us
where the time goes in v6:
time: 20.1 us; the launch traced here: 19.9 us
  Pallas kernels  16.7 us (83%)
  local copies, waits for them, and re-layouts  3.17 us (16%)
    pallas_call x1, Pallas kernels, local(): pl.pallas_call(functools.partial(gather, time_count, group_count, row_sha...  16.7 us
    unnamed x7, local copies, waits for them, and re-layouts  3.17 us

profile of v6, /device:TPU:0, one launch (start us, length us, event | category | flops | bytes accessed | tf_op | source)
XLA Modules:
  0.0 19.9 jit_solution(6612297089233432531)
XLA Ops:
  0.0 0.0 copy-start
  0.0 0.8 %copy-done = f32[64,256]{1,0:T(8,128)S(1)} copy-done((f32[64,256]{1,0:T(8,128)S(1)}, f32[64,256]{1,0:T(8,128)}, u32[]{:S(2)}) %copy-start) | copy-done | bytes 65560
  0.8 0.0 copy-start.1
  0.8 0.7 %copy-done.1 = s32[2,4]{1,0:T(2,128)S(1)} copy-done((s32[2,4]{1,0:T(2,128)S(1)}, s32[2,4]{1,0:T(2,128)}, u32[]{:S(2)}) %copy-start.1) | copy-done | bytes 56
  1.5 0.0 copy-start.2
  1.5 0.7 %copy-done.2 = f32[129]{0:T(256)S(1)} copy-done((f32[129]{0:T(256)S(1)}, f32[129]{0:T(256)}, u32[]{:S(2)}) %copy-start.2) | copy-done | bytes 540
  2.2 16.7 %shard_map.37 = bf16[2,1,16,16448]{3,2,1,0:T(8,128)(2,1)S(1)} custom-call(s32[2,4]{1,0:T(2,128)S(1)} %copy-done.1, f32[1,129]{1,0:T(1,128)S(1)} %bitcast.1, f32[64,256]{1,0:T(8,128)S(1)} %copy-done), custom_call_target="tpu_custom_call" | custom-call | tf_op jit(solution)/shard_map/pallas_call | solution.py:231
  18.9 1.0 %copy.5 = bf16[2,1,16,16448]{3,2,1,0:T(8,128)(2,1)} copy(bf16[2,1,16,16448]{3,2,1,0:T(8,128)(2,1)S(1)} %shard_map.37) | data formatting | bytes 2105344
Async XLA Ops:
  0.0 0.8 %copy-start = (f32[64,256]{1,0:T(8,128)S(1)}, f32[64,256]{1,0:T(8,128)}, u32[]{:S(2)}) copy-start(f32[64,256]{1,0:T(8,128)} %records_hbm.1) | copy-start | bytes 196612
  0.8 0.7 %copy-start.1 = (s32[2,4]{1,0:T(2,128)S(1)}, s32[2,4]{1,0:T(2,128)}, u32[]{:S(2)}) copy-start(s32[2,4]{1,0:T(2,128)} %matchings_hbm.1) | copy-start | bytes 100
  1.5 0.7 %copy-start.2 = (f32[129]{0:T(256)S(1)}, f32[129]{0:T(256)}, u32[]{:S(2)}) copy-start(f32[129]{0:T(256)} %param.4) | copy-start | bytes 1552

commit v7 on v6

--- a/solution.py
+++ b/solution.py
@@ -127,6 +127,8 @@
     for load in loads:
         load.wait()
     every_ref[chan_at, time_at] = records_ref[...].astype(jnp.bfloat16)
+    samples_dev = every_ref.shape[3]
+    prepared = prepare(taps_ref, taps_row, samples_dev)
     pl.semaphore_wait(barrier, len(peers))
 
     sent = []
@@ -161,14 +163,12 @@
         for chan_to in others + cross:
             push(chan_at, time_from, {"chan": chan_to})
         push(chan_at, time_from, sibling)
-    samples_dev = every_ref.shape[3]
     group_ch, match_count = every_ref.shape[2], matchings_ref.shape[0]
     samples = time_count * samples_dev
     depth, width = samples + MAXLAG, samples + 2 * MAXLAG
     rows = -(-row_share // 16) * 16
     row_at = time_at * row_share
     start = pl.multiple_of(row_at // rows * rows, rows)
-    prepared = prepare(taps_ref, taps_row, samples_dev)
     own = jnp.concatenate(
         [every_ref[chan_at, at, pl.ds(start, rows), :] for at in range(time_count)], axis=1
     )
@@ -246,7 +246,7 @@
             pltpu.SemaphoreType.DMA((sends,)),
             pltpu.SemaphoreType.DMA((group_count, time_count)),
         ],
-        compiler_params=pltpu.CompilerParams(vmem_limit_bytes=40<<20, collective_id=0, has_side_effects=True),
+        compiler_params=pltpu.CompilerParams(collective_id=0, has_side_effects=True),
     )(matchings, fir_taps.reshape(1, -1), records)
 
 

time: 20.1 us -> 19.7 us (0.980)
  local copies, waits for them, and re-layouts: 3.17 us -> 2.27 us
  Pallas kernels: 16.7 us -> 17.3 us
    unnamed x7 -> x1, local copies, waits for them, and re-layouts: 3.17 us -> 2.27 us
    pallas_call x1, Pallas kernels: 16.7 us -> 17.3 us  [local(): pl.pallas_call(functools.partial(gather, time_count, group_count, row_sha...]
where the time goes in v7:
time: 19.7 us; the launch traced here: 19.6 us
  Pallas kernels  17.3 us (88%)
  local copies, waits for them, and re-layouts  2.27 us (12%)
    pallas_call x1, Pallas kernels, local(): pl.pallas_call(functools.partial(gather, time_count, group_count, row_sha...  17.3 us
    unnamed x1, local copies, waits for them, and re-layouts  2.27 us

profile of v7, /device:TPU:0, one launch (start us, length us, event | category | flops | bytes accessed | tf_op | source)
XLA Modules:
  0.0 19.6 jit_solution(5767445919990840046)
XLA Ops:
  0.0 17.3 %shard_map.37 = bf16[2,1,16,16448]{3,2,1,0:T(8,128)(2,1)} custom-call(s32[2,4]{1,0:T(2,128)} %matchings_hbm.1, f32[1,129]{1,0:T(1,128)} %bitcast.1, f32[64,256]{1,0:T(8,128)} %records_hbm.1), custom_call_target="tpu_custom_call" | custom-call | tf_op jit(solution)/shard_map/pallas_call | solution.py:231
  17.3 2.3 %copy.5 = bf16[2,1,16,16448]{3,2,1,0:T(8,128)(2,1)} copy(bf16[2,1,16,16448]{3,2,1,0:T(8,128)(2,1)} %shard_map.37) | data formatting | bytes 2105344
